TPU v7x, 32 devices: a whole 2x2x4 slice. The times are simulated.
32 devices in a mesh: sub: 16 (over z, y, x), mode: 2 (over core).
Axes of the slice: x: 2, y: 2, z: 4, core: 2. Of those that a mesh axis runs over, the one named last changes fastest.
Arguments:
- coupling: bfloat16 [1024, 64, 128], P('sub'), may hold values from -0.5 to 0.5
- coupling_pairs: int32 [1024, 2], P('sub'), may hold values from 0 to 3, as said below
- modes: bfloat16 [1024, 256, 256], P('sub', None, 'mode'), may hold values from -6 to 6
- mode_weights: bfloat16 [1024, 256], P('sub', 'mode'), may hold values from 0 to 1, as said below
- parent_of: int32 [1024, 1], P('sub'), may hold values from 0 to 15; in each aligned block of 64 rows (0 to 63, 64 to 127, ...) at most 8 rows name the same one
- row_block: int32 [1024], P('sub'), may hold values from 0 to 7
- parent_modes: bfloat16 [16, 512, 256], P('sub'), may hold values from -1 to 1
- parent_eigs: float32 [16, 256], P('sub'), may hold values from 0.02 to 0.5
Outputs:
- strengths: float32 [1024, 256], P('sub', 'mode')
Inputs may be any that keep to these rules, and one draw needn't show every extreme that they name: `coupling_pairs`: within each child the 2 block indices are distinct. `parent_of`: the 64 children of one index of sub name any one parent at most 8 times; some parent is named exactly 8 times by some index's children. `mode_weights`: Positive.
All inputs are finite; a program needn't handle non-finite values.
Results may differ from a plain program's by a relative error of at most 0.0015.
Values may be sent and summed in bfloat16 or wider, within the bound.
A program may use at most 128 MiB of HBM per device.

v0:
```python
import jax
import jax.numpy as jnp
from jax import lax
from jax.sharding import PartitionSpec as P

M = 256
MP = 256
BLK = 64
CH_DEV = 64


def pick_blocks(modes, coupling_pairs):
    child_count, interface_rows, mode_cols = modes.shape
    blocks = modes.reshape(child_count, interface_rows // BLK, BLK, mode_cols)
    selector = (
        coupling_pairs[:, :, None]
        == jnp.arange(interface_rows // BLK, dtype=jnp.int32)[None, None, :]
    ).astype(jnp.bfloat16)
    picked = jnp.einsum(
        "skb,sbim->skim", selector, blocks, preferred_element_type=jnp.float32
    ).astype(jnp.bfloat16)
    return picked.reshape(child_count, coupling_pairs.shape[1] * BLK, mode_cols)


def weighted_records(coupling_rows, picked, weights):
    record = jnp.einsum("sij,sjm->sim", coupling_rows, picked, preferred_element_type=jnp.float32)
    return (record * weights[:, None, :].astype(jnp.float32)).astype(jnp.bfloat16)


def to_slots(values, slot_index, slot_count):
    empty = jnp.zeros((slot_count,) + values.shape[1:], values.dtype)
    return empty.at[slot_index].set(values)


def per_device(
    coupling, coupling_pairs, modes, mode_weights, parent_of, row_block, parent_modes, parent_eigs
):
    sub_count = lax.axis_size("sub")
    child_count = coupling.shape[0]
    mode_cols = modes.shape[2]
    capacity = max(2, 2 * child_count // sub_count)
    slot_count = sub_count * capacity
    owner = parent_of[:, 0]
    order_ids = jnp.arange(child_count, dtype=jnp.int32)
    earlier = (owner[:, None] == owner[None, :]) & (order_ids[None, :] < order_ids[:, None])
    position = jnp.sum(earlier.astype(jnp.int32), axis=1)
    slot_index = owner * capacity + position
    picked = pick_blocks(modes, coupling_pairs)
    row_send = to_slots(row_block, slot_index, slot_count).reshape(sub_count, capacity)
    record = weighted_records(coupling, picked, mode_weights)
    record_send = to_slots(record, slot_index, slot_count).reshape(
        sub_count, capacity, BLK, mode_cols
    )
    record_recv, row_recv = (
        lax.all_to_all(record_send, "sub", split_axis=0, concat_axis=0, tiled=True),
        lax.all_to_all(row_send, "sub", split_axis=0, concat_axis=0, tiled=True),
    )
    records = record_recv.reshape(slot_count, BLK, mode_cols)
    row_index = row_recv.reshape(slot_count)
    sep_blocks = parent_modes.shape[1] // BLK
    parent_blocks = parent_modes[0].reshape(sep_blocks, BLK, MP)
    group_size = min(64, slot_count)
    group_count = slot_count // group_size
    record_groups = records.reshape(group_count, group_size, BLK, mode_cols)
    row_groups = row_index.reshape(group_count, group_size)

    def project(gram_sum, members):
        record_part, row_part = members
        selector = (row_part[:, None] == jnp.arange(sep_blocks, dtype=jnp.int32)[None, :]).astype(
            jnp.bfloat16
        )
        parent_rows = jnp.einsum(
            "sb,bik->sik", selector, parent_blocks, preferred_element_type=jnp.float32
        ).astype(jnp.bfloat16)
        projected = jnp.einsum(
            "sik,sim->skm", parent_rows, record_part, preferred_element_type=jnp.float32
        ).astype(jnp.bfloat16)
        term = jnp.einsum("skm,slm->kl", projected, projected, preferred_element_type=jnp.float32)
        return (gram_sum + term, projected)

    gram_sum, projected_all = lax.scan(
        project, jnp.zeros((MP, MP), jnp.float32), (record_groups, row_groups)
    )
    gram_sum = lax.psum(gram_sum, "mode")
    pencil = jnp.diag(parent_eigs[0]) + gram_sum / (CH_DEV * M)
    factor = jnp.linalg.cholesky(pencil)
    identity = jnp.eye(MP, dtype=pencil.dtype)
    inverse = lax.linalg.triangular_solve(factor, identity, left_side=True, lower=True).astype(
        jnp.bfloat16
    )

    def strength(projected):
        rotated = jnp.einsum("kl,slm->skm", inverse, projected, preferred_element_type=jnp.float32)
        return jnp.sum(rotated * rotated, axis=1) / MP

    slot_values = lax.map(strength, projected_all).reshape(sub_count, capacity, mode_cols)
    returned = lax.all_to_all(slot_values, "sub", split_axis=0, concat_axis=0, tiled=True)
    return returned.reshape(slot_count, mode_cols)[slot_index]


def solution(mesh):
    in_specs = (
        P("sub", None, None),
        P("sub", None),
        P("sub", None, "mode"),
        P("sub", "mode"),
        P("sub", None),
        P("sub"),
        P("sub", None, None),
        P("sub", None),
    )
    out_specs = P("sub", "mode")
    return jax.shard_map(
        per_device, mesh=mesh, in_specs=in_specs, out_specs=out_specs, check_vma=False
    )
```

profile of v0, /device:TPU:0, one launch (start us, length us, event | category | flops | bytes accessed | tf_op | source)
XLA Modules:
  0.0 229.0 jit_solution(5430570650498612388)
XLA Ops:
  6.5 0.9 convert_reduce_fusion
  8.1 0.9 scatter_custom_fusion
  9.7 8.3 %all-to-all-start = ((s32[16,1,8]{2,1,0:T(1,128)}), s32[16,1,8]{2,1,0:T(1,128)S(1)}, u32[]{:S(2)}, u32[]{:S(2)}) async-start(s32[16,1,8]{2,1,0:T(1,128)} %bitcast.6), calls=%async_computation | async-start | bytes 16384 | tf_op jit(solution)/shard_map/all_to_all | solution.py:56
  18.9 5.6 %fusion.15 = bf16[64,2,64,128]{3,1,2,0:T(2,128)(2,1)S(1)} fusion(bf16[64,4,64,128]{3,2,1,0:T(8,128)(2,1)} %bitcast.113, s32[64,2]{1,0:T(8,128)S(1)} %copy.57), kind=kOutput, calls=%fused_computation.27 | convolution fusion | flops 9437696 | bytes 6291968 | tf_op jit(solution)/shard_map/skb,sbim->skim/dot_general | solution.py:19
  25.2 1.7 fusion.18
  27.4 6.2 %scatter_fusion = bf16[128,64,128]{2,1,0:T(8,128)(2,1)S(1)} fusion(bf16[128,64,128]{2,1,0:T(8,128)(2,1)S(1)} %broadcast_in_dim.55, s32[64]{0:T(128)S(1)} %fusion.31, bf16[64,64,128]{2,1,0:T(8,128)(2,1)} %fusion.18), kind=kCustom, calls=%fused_computation.2 | custom fusion | bytes 3145984 | tf_op jit(solution)/shard_map/scatter | solution.py:32
  33.6 1.4 copy-done.1
  35.0 6.9 %all-to-all-start.1 = ((bf16[16,8,64,128]{3,2,1,0:T(8,128)(2,1)}), bf16[16,8,64,128]{3,2,1,0:T(8,128)(2,1)S(1)}, u32[]{:S(2)}, u32[]{:S(2)}) async-start(bf16[16,8,64,128]{3,2,1,0:T(8,128)(2,1)} %bitcast.107), calls=%async_computation.1 | async-start | bytes 4194304 | tf_op jit(solution)/shard_map/all_to_all | solution.py:55
  42.0 1.1 copy.60
  44.4 40.2 %all-to-all-done.1 = bf16[16,8,64,128]{3,2,1,0:T(8,128)(2,1)S(1)} async-done(((bf16[16,8,64,128]{3,2,1,0:T(8,128)(2,1)}), bf16[16,8,64,128]{3,2,1,0:T(8,128)(2,1)S(1)}, u32[]{:S(2)}, u32[]{:S(2)}) %all-to-all-start.1) | async-done | bytes 2097184 | tf_op jit(solution)/shard_map/all_to_all | solution.py:55
  84.6 24.0 %while.26 = (s32[]{:T(128)}, f32[256,256]{1,0:T(8,128)}, bf16[2,64,256,128]{3,2,1,0:T(8,128)(2,1)}, s32[2,64]{1,0:T(2,128)S(1)}, bf16[8,64,256]{2,0,1:T(8,128)(2...) while((s32[]{:T(128)}, f32[256,256]{1,0:T(8,128)}, ...), condition=%wide.region_4.5_spmd.clone, body=%wide.region_3.4_spmd.clone.sunk | while | flops 1362231808 | bytes 18614116 | solution.py:81
  85.4 5.7 %bitcast_dynamic-update-slice_fusion.8 = (bf16[2,64,256,128]{3,2,1,0:T(8,128)(2,1)}, bf16[64,256,128]{2,1,0:T(8,128)(2,1)}) fusion(bf16[2,64,256,128]{3,2,1,0:T(8,128)(2,1)} %get-tuple-element.287, s32[]{:T(128)} %get-tuple-element.285, bf16[2,64,64,128]{3,2,1,0:T(8,128)(2,1)S(1)} %get-tuple-element.298, ...), kind=kOutput, calls=%fused_computation.11.clone.1 | convolution fusion | flops 270532608 | bytes 11535360 | tf_op jit(solution)/shard_map/while/body/eval_jaxpr/sik,sim->skm/dot_general | solution.py:75
  91.1 5.5 %fusion.62 = f32[256,256]{1,0:T(8,128)} fusion(bf16[64,256,128]{2,1,0:T(8,128)(2,1)} %get-tuple-element.275, f32[256,256]{1,0:T(8,128)} %get-tuple-element.286, pred[]{:T(512)S(6)} %compare.26), kind=kOutput, calls=%fused_computation.16.clone.1 | convolution fusion | flops 1073872896 | bytes 4718593 | tf_op jit(solution)/shard_map/while/body/eval_jaxpr/skm,slm->kl/dot_general | solution.py:78
  97.3 5.8 %bitcast_dynamic-update-slice_fusion.8 = (bf16[2,64,256,128]{3,2,1,0:T(8,128)(2,1)}, bf16[64,256,128]{2,1,0:T(8,128)(2,1)}) fusion(bf16[2,64,256,128]{3,2,1,0:T(8,128)(2,1)} %get-tuple-element.287, s32[]{:T(128)} %get-tuple-element.285, bf16[2,64,64,128]{3,2,1,0:T(8,128)(2,1)S(1)} %get-tuple-element.298, ...), kind=kOutput, calls=%fused_computation.11.clone.1 | convolution fusion | flops 270532608 | bytes 11535360 | tf_op jit(solution)/shard_map/while/body/eval_jaxpr/sik,sim->skm/dot_general | solution.py:75
  103.1 5.5 %fusion.62 = f32[256,256]{1,0:T(8,128)} fusion(bf16[64,256,128]{2,1,0:T(8,128)(2,1)} %get-tuple-element.275, f32[256,256]{1,0:T(8,128)} %get-tuple-element.286, pred[]{:T(512)S(6)} %compare.26), kind=kOutput, calls=%fused_computation.16.clone.1 | convolution fusion | flops 1073872896 | bytes 4718593 | tf_op jit(solution)/shard_map/while/body/eval_jaxpr/skm,slm->kl/dot_general | solution.py:78
  108.6 1.8 copy.61
  110.5 22.5 %all-reduce.3.cloned.1.call-done = f32[256,256]{0,1:T(8,128)} async-done(((f32[256,256]{0,1:T(8,128)}), f32[256,256]{0,1:T(8,128)}) %all-reduce.3.cloned.1.call-update) | async-done | bytes 262160 | tf_op jit(solution)/shard_map/psum | solution.py:84
  133.0 1.0 multiply_add_fusion
  134.1 1.0 fusion.19
  135.2 11.7 %cholesky.49 = f32[128,128]{1,0:T(8,128)S(1)} custom-call(f32[128,128]{1,0:T(8,128)S(1)} %cholesky.115), custom_call_target="Cholesky" | custom-call | tf_op jit(solution)/shard_map/jit(cholesky)/cholesky | solution.py:86
  146.9 9.8 %custom-call.14 = f32[1,128,128]{1,2,0:T(8,128)S(1)} custom-call(f32[1,128,128]{2,1,0:T(8,128)S(1)} %get-tuple-element.177), custom_call_target="InvertDiagBlocksLowerTriangular" | custom-call | tf_op jit(solution)/shard_map/jit(cholesky)/cholesky | solution.py:86
  157.2 11.7 %cholesky.103 = f32[128,128]{1,0:T(8,128)S(1)} custom-call(f32[128,128]{1,0:T(8,128)S(1)} %convolution_subtract_fusion.1), custom_call_target="Cholesky" | custom-call | tf_op jit(solution)/shard_map/jit(cholesky)/cholesky | solution.py:86
  171.3 4.0 %while.25 = (s32[]{:T(128)}, f32[256,256]{0,1:T(8,128)S(1)}, s32[2,2]{1,0:T(2,128)S(1)}, f32[2,128,128]{2,1,0:T(8,128)S(1)}, s32[]{:T(128)}) while((s32[]{:T(128)}, f32[256,256]{0,1:T(8,128)S(1)}, s32[2,2]{1,0:T(2,128)S(1)}, f32[2,128,128]{2,1,0:T(8,128)S(1)}, s32[]{:T(128)}) %tuple.70), condition=%wide.while_cond, body=%wide.while_body.sunk | while | flops 2 | bytes 393321 | solution.py:88
  171.8 1.3 dynamic-slice.7
  173.8 1.3 dynamic-slice.7
  175.3 19.9 %custom-call.15 = f32[2,128,128]{1,2,0:T(8,128)S(1)} custom-call(f32[2,128,128]{2,1,0:T(8,128)S(1)} %get-tuple-element.70), custom_call_target="InvertDiagBlocksLowerTriangular" | custom-call | tf_op jit(solution)/shard_map/triangular_solve | solution.py:88
  196.2 10.5 %while.24 = (s32[]{:T(128)}, f32[2,64,128]{2,1,0:T(8,128)}, bf16[2,64,256,128]{3,2,1,0:T(8,128)(2,1)}, bf16[256,256]{1,0:T(8,128)(2,1)S(1)}, s32[]{:T(128)}) while((s32[]{:T(128)}, f32[2,64,128]{2,1,0:T(8,128)}, bf16[2,64,256,128]{3,2,1,0:T(8,128)(2,1)}, bf16[256,256]{1,0:T(8,128)(2,1)S(1)}, s32[]{:T(128)}) %tuple.73), condition=%wide.region_12.13_spmd, body=%wide.region_10.12_spmd.sunk | while | flops 1077936128 | bytes 4424765 | solution.py:96
  196.2 4.6 %multiply_reduce_fusion.2 = f32[64,128]{1,0:T(8,128)S(1)} fusion(bf16[2,64,256,128]{3,2,1,0:T(8,128)(2,1)} %get-tuple-element.328, s32[]{:T(128)} %get-tuple-element.321, bf16[256,256]{1,0:T(8,128)(2,1)S(1)} %get-tuple-element.329), kind=kOutput, calls=%fused_computation.3.clone.1 | convolution fusion | flops 1077927936 | bytes 4358656 | tf_op jit(solution)/shard_map/while/body/eval_jaxpr/kl,slm->skm/dot_general | solution.py:93
  201.4 4.6 %multiply_reduce_fusion.2 = f32[64,128]{1,0:T(8,128)S(1)} fusion(bf16[2,64,256,128]{3,2,1,0:T(8,128)(2,1)} %get-tuple-element.328, s32[]{:T(128)} %get-tuple-element.321, bf16[256,256]{1,0:T(8,128)(2,1)S(1)} %get-tuple-element.329), kind=kOutput, calls=%fused_computation.3.clone.1 | convolution fusion | flops 1077927936 | bytes 4358656 | tf_op jit(solution)/shard_map/while/body/eval_jaxpr/kl,slm->skm/dot_general | solution.py:93
  206.6 6.8 %all-to-all-start.2 = ((f32[16,8,128]{2,1,0:T(8,128)}), f32[16,8,128]{2,1,0:T(8,128)S(1)}, u32[]{:S(2)}, u32[]{:S(2)}) async-start(f32[16,8,128]{2,1,0:T(8,128)} %bitcast.21), calls=%async_computation.2 | async-start | bytes 131072 | tf_op jit(solution)/shard_map/all_to_all | solution.py:97
  213.5 7.5 %all-to-all-done.2 = f32[16,8,128]{2,1,0:T(8,128)S(1)} async-done(((f32[16,8,128]{2,1,0:T(8,128)}), f32[16,8,128]{2,1,0:T(8,128)S(1)}, u32[]{:S(2)}, u32[]{:S(2)}) %all-to-all-start.2) | async-done | bytes 65568 | tf_op jit(solution)/shard_map/all_to_all | solution.py:97
  221.0 1.2 gather_fusion
  (59 shorter events, 11.6 us)
Async XLA Ops:
  6.5 18.6 %copy-start = (bf16[64,64,128]{2,1,0:T(8,128)(2,1)S(1)}, bf16[64,64,128]{2,1,0:T(8,128)(2,1)}, u32[]{:S(2)}) copy-start(bf16[64,64,128]{2,1,0:T(8,128)(2,1)} %param.12) | copy-start | bytes 3145732
  9.7 23.8 %all-to-all-start = ((s32[16,1,8]{2,1,0:T(1,128)}), s32[16,1,8]{2,1,0:T(1,128)S(1)}, u32[]{:S(2)}, u32[]{:S(2)}) async-start(s32[16,1,8]{2,1,0:T(1,128)} %bitcast.6), calls=%async_computation | async-start | bytes 16384 | tf_op jit(solution)/shard_map/all_to_all | solution.py:56
  24.5 0.7 copy-start.2
  33.6 1.4 copy-start.1
  35.0 49.6 %all-to-all-start.1 = ((bf16[16,8,64,128]{3,2,1,0:T(8,128)(2,1)}), bf16[16,8,64,128]{3,2,1,0:T(8,128)(2,1)S(1)}, u32[]{:S(2)}, u32[]{:S(2)}) async-start(bf16[16,8,64,128]{3,2,1,0:T(8,128)(2,1)} %bitcast.107), calls=%async_computation.1 | async-start | bytes 4194304 | tf_op jit(solution)/shard_map/all_to_all | solution.py:55
  41.9 91.1 %all-reduce.3.cloned.1.call-start = ((), (), s32[]{:S(2)}) async-start(), calls=%async_computation.3 | async-start | bytes 524288 | tf_op jit(solution)/shard_map/psum | solution.py:84
  84.6 48.4 %copy-start.3 = (f32[1,256]{1,0:T(1,128)S(1)}, f32[1,256]{1,0:T(1,128)}, u32[]{:S(2)}) copy-start(f32[1,256]{1,0:T(1,128)} %param.19) | copy-start | bytes 3076
  206.6 14.4 %all-to-all-start.2 = ((f32[16,8,128]{2,1,0:T(8,128)}), f32[16,8,128]{2,1,0:T(8,128)S(1)}, u32[]{:S(2)}, u32[]{:S(2)}) async-start(f32[16,8,128]{2,1,0:T(8,128)} %bitcast.21), calls=%async_computation.2 | async-start | bytes 131072 | tf_op jit(solution)/shard_map/all_to_all | solution.py:97
Sparse Core Ops, SparseCore 0:
  110.5 22.4 all-reduce.2
where the time goes:
time: 230 us; the launch traced here: 229 us
  waiting for transfers between devices  70.3 us (31%)
  other arithmetic  59.4 us (26%)
  matrix products  41.9 us (18%)
  starting transfers between devices  22.1 us (10%)
  local copies, waits for them, and re-layouts  20.3 us (9%)
  between operations  14.9 us (6%)
    all_to_all x1, waiting for transfers between devices, per_device(): lax.all_to_all(record_send, 'sub', split_axis=0, concat_axis=0, tiled=True)  40.2 us
    another operation x6, other arithmetic, per_device(): factor = jnp.linalg.cholesky(pencil)  34 us
    psum x1, waiting for transfers between devices, per_device(): gram_sum = lax.psum(gram_sum, 'mode')  22.5 us
    another operation x4, other arithmetic, per_device(): lax.linalg.triangular_solve(factor, identity, left_side=True, lower=True)  19.9 us
    dot_general x2, matrix products, project(): jnp.einsum('sik,sim->skm', parent_rows, record_part, preferred_element_ty...  11.5 us
    dot_general x2, matrix products, project(): jnp.einsum('skm,slm->kl', projected, projected, preferred_element_type=jn...  11 us
    dot_general x2, matrix products, strength(): jnp.einsum('kl,slm->skm', inverse, projected, preferred_element_type=jnp....  9.22 us
    all_to_all x1, starting transfers between devices, per_device(): lax.all_to_all(row_send, 'sub', split_axis=0, concat_axis=0, tiled=True)  8.34 us
  transfers between devices with their start and end apart: 4, of which 3 were waited for; matrix products, arithmetic and copies ran while one was open for 8% of the time, Pallas kernels for 0%

commit v1 on v0

--- a/solution.py
+++ b/solution.py
@@ -7,6 +7,22 @@
 MP = 256
 BLK = 64
 CH_DEV = 64
+
+
+def obtain_leaves(page, on_dim, my_data):
+    local_out = page.shape
+    current_value = page.reshape(
+        *local_out[:on_dim], my_data, local_out[on_dim] // my_data, *local_out[on_dim + 1 :]
+    )
+    right_arr = jnp.moveaxis(current_value, on_dim, 0)
+    return right_arr
+
+
+def _close_samples_all(vals, row_dim):
+    odd = list(vals.shape[1:])
+    odd[row_dim] *= vals.shape[0]
+    placed = jnp.moveaxis(vals, 0, row_dim).reshape(odd)
+    return placed
 
 
 def pick_blocks(modes, coupling_pairs):
@@ -51,8 +67,26 @@
     record_send = to_slots(record, slot_index, slot_count).reshape(
         sub_count, capacity, BLK, mode_cols
     )
+
+    def sheet_launch(local, mesh_name, load, tile_in):
+        upper = jax.lax.axis_size(mesh_name)
+        part_now = jax.lax.axis_index(mesh_name)
+        met_up, w1 = (upper, part_now)
+        carry_out = obtain_leaves(local, load, met_up)
+        samples = [carry_out[w1]]
+        for idx in range(1, met_up):
+            o_now = carry_out[(w1 + idx) % met_up]
+            kept_arr = jax.lax.ppermute(
+                o_now, axis_name=mesh_name, perm=[(u, (u + idx) % met_up) for u in range(met_up)]
+            )
+            samples.append(kept_arr)
+        arr_out = jnp.stack(samples, 0)
+        carry_out = arr_out[(w1 - jnp.arange(met_up)) % met_up]
+        w2 = _close_samples_all(carry_out, tile_in)
+        return w2
+
     record_recv, row_recv = (
-        lax.all_to_all(record_send, "sub", split_axis=0, concat_axis=0, tiled=True),
+        sheet_launch(record_send, mesh_name="sub", load=0, tile_in=0),
         lax.all_to_all(row_send, "sub", split_axis=0, concat_axis=0, tiled=True),
     )
     records = record_recv.reshape(slot_count, BLK, mode_cols)

time: 230 us -> 241 us (1.048)
  waiting for transfers between devices: 70.3 us -> 49.1 us
  starting transfers between devices: 22.1 us -> 42.8 us
  local copies, waits for them, and re-layouts: 20.3 us -> 32.2 us
    all_to_all x1 -> x0, waiting for transfers between devices: 40.2 us -> none  [per_device(): lax.all_to_all(record_send, 'sub', split_axis=0, concat_axis=0, tiled=True)]
    ppermute x0 -> x15, starting transfers between devices: none -> 30.4 us  [sheet_launch(): jax.lax.ppermute(o_now, axis_name=mesh_name, perm=[(u, (u + idx) % met_up...]
    ppermute x0 -> x15, waiting for transfers between devices: none -> 10.6 us  [sheet_launch(): jax.lax.ppermute(o_now, axis_name=mesh_name, perm=[(u, (u + idx) % met_up...]
    all_to_all x1, waiting for transfers between devices: 0.01 us -> 7.46 us  [per_device(): lax.all_to_all(row_send, 'sub', split_axis=0, concat_axis=0, tiled=True)]
    unnamed x10 -> x30, local copies, waits for them, and re-layouts: 3.39 us -> 10.3 us
    all_to_all x1 -> x0, starting transfers between devices: 6.91 us -> none  [per_device(): lax.all_to_all(record_send, 'sub', split_axis=0, concat_axis=0, tiled=True)]
    all_to_all x1, starting transfers between devices: 8.34 us -> 5.51 us  [per_device(): lax.all_to_all(row_send, 'sub', split_axis=0, concat_axis=0, tiled=True)]
    gather x0 -> x1, local copies, waits for them, and re-layouts: none -> 2.54 us  [sheet_launch(): carry_out = arr_out[(w1 - jnp.arange(met_up)) % met_up]]
  transfers between devices with their start and end apart: 4 -> 18, of which waited for: 3 -> 6; matrix products, arithmetic and copies ran while one was open for 8% -> 5% of each run, Pallas kernels for 0% -> 0%
where the time goes in v1:
time: 241 us; the launch traced here: 240 us
  other arithmetic  59.5 us (25%)
  waiting for transfers between devices  49.1 us (20%)
  starting transfers between devices  42.8 us (18%)
  matrix products  41.8 us (17%)
  local copies, waits for them, and re-layouts  32.2 us (13%)
  between operations  14.9 us (6%)
    another operation x6, other arithmetic, per_device(): factor = jnp.linalg.cholesky(pencil)  34 us
    ppermute x15, starting transfers between devices, sheet_launch(): jax.lax.ppermute(o_now, axis_name=mesh_name, perm=[(u, (u + idx) % met_up...  30.4 us
    psum x1, waiting for transfers between devices, per_device(): gram_sum = lax.psum(gram_sum, 'mode')  23.5 us
    another operation x4, other arithmetic, per_device(): lax.linalg.triangular_solve(factor, identity, left_side=True, lower=True)  19.9 us
    dot_general x2, matrix products, project(): jnp.einsum('sik,sim->skm', parent_rows, record_part, preferred_element_ty...  11.5 us
    dot_general x2, matrix products, project(): jnp.einsum('skm,slm->kl', projected, projected, preferred_element_type=jn...  10.9 us
    ppermute x15, waiting for transfers between devices, sheet_launch(): jax.lax.ppermute(o_now, axis_name=mesh_name, perm=[(u, (u + idx) % met_up...  10.6 us
    unnamed x30, local copies, waits for them, and re-layouts  10.3 us
  transfers between devices with their start and end apart: 18, of which 6 were waited for; matrix products, arithmetic and copies ran while one was open for 5% of the time, Pallas kernels for 0%

profile of v1, /device:TPU:0, one launch (start us, length us, event | category | flops | bytes accessed | tf_op | source)
XLA Modules:
  0.0 240.4 jit_solution(16793259946870694766)
XLA Ops:
  8.9 5.6 %fusion.15 = bf16[64,2,64,128]{3,1,2,0:T(2,128)(2,1)S(1)} fusion(bf16[64,4,64,128]{3,2,1,0:T(8,128)(2,1)} %bitcast.177, s32[64,2]{1,0:T(8,128)S(1)} %copy.57), kind=kOutput, calls=%fused_computation.28 | convolution fusion | flops 9437696 | bytes 6291968 | tf_op jit(solution)/shard_map/skb,sbim->skim/dot_general | solution.py:35
  17.4 6.2 %scatter_fusion = bf16[128,64,128]{2,1,0:T(8,128)(2,1)S(1)} fusion(bf16[128,64,128]{2,1,0:T(8,128)(2,1)S(1)} %broadcast_in_dim.56, s32[64]{0:T(128)S(1)} %fusion.32, bf16[64,64,128]{2,1,0:T(8,128)(2,1)} %fusion.18), kind=kCustom, calls=%fused_computation.3 | custom fusion | bytes 3145984 | tf_op jit(solution)/shard_map/scatter | solution.py:48
  25.2 3.0 %collective-permute-start = (bf16[1,8,64,128]{3,2,1,0:T(8,128)(2,1)}, bf16[1,8,64,128]{3,2,1,0:T(8,128)(2,1)S(1)}, u32[]{:S(2)}, u32[]{:S(2)}) collective-permute-start(bf16[1,8,64,128]{3,2,1,0:T(8,128)(2,1)} %get-tuple-element.190), channel_id=1, source_target_pairs={{0,2},{2,4},{4,6},{6,8},{8,10},{10,12},{12,14},{14,16},{16,18},{18... | collective-permute-start | bytes 393224 | tf_op jit(solution)/shard_map/ppermute | solution.py:79
  29.7 2.4 %collective-permute-start.2 = (bf16[1,8,64,128]{3,2,1,0:T(8,128)(2,1)}, bf16[1,8,64,128]{3,2,1,0:T(8,128)(2,1)S(1)}, u32[]{:S(2)}, u32[]{:S(2)}) collective-permute-start(bf16[1,8,64,128]{3,2,1,0:T(8,128)(2,1)} %get-tuple-element.188), channel_id=1, source_target_pairs={{0,6},{2,8},{4,10},{6,12},{8,14},{10,16},{12,18},{14,20},{16,22},{... | collective-permute-start | bytes 393224 | tf_op jit(solution)/shard_map/ppermute | solution.py:79
  37.0 5.5 %all-to-all-start = ((s32[16,1,8]{2,1,0:T(1,128)}), s32[16,1,8]{2,1,0:T(1,128)S(1)}, u32[]{:S(2)}, u32[]{:S(2)}) async-start(s32[16,1,8]{2,1,0:T(1,128)} %bitcast.6), calls=%async_computation | async-start | bytes 16384 | tf_op jit(solution)/shard_map/all_to_all | solution.py:90
  42.7 7.5 %all-to-all-done = s32[16,1,8]{2,1,0:T(1,128)S(1)} async-done(((s32[16,1,8]{2,1,0:T(1,128)}), s32[16,1,8]{2,1,0:T(1,128)S(1)}, u32[]{:S(2)}, u32[]{:S(2)}) %all-to-all-start) | async-done | bytes 544 | tf_op jit(solution)/shard_map/all_to_all | solution.py:90
  52.7 2.4 %collective-permute-start.6 = (bf16[1,8,64,128]{3,2,1,0:T(8,128)(2,1)}, bf16[1,8,64,128]{3,2,1,0:T(8,128)(2,1)S(1)}, u32[]{:S(2)}, u32[]{:S(2)}) collective-permute-start(bf16[1,8,64,128]{3,2,1,0:T(8,128)(2,1)} %get-tuple-element.184), channel_id=1, source_target_pairs={{0,14},{2,16},{4,18},{6,20},{8,22},{10,24},{12,26},{14,28},{16,30}... | collective-permute-start | bytes 393224 | tf_op jit(solution)/shard_map/ppermute | solution.py:79
  60.0 2.3 collective-permute-start.9
  63.0 6.9 %collective-permute-done.5 = bf16[1,8,64,128]{3,2,1,0:T(8,128)(2,1)S(1)} collective-permute-done((bf16[1,8,64,128]{3,2,1,0:T(8,128)(2,1)}, bf16[1,8,64,128]{3,2,1,0:T(8,128)(2,1)S(1)}, u32[]{:S(2)}, u32[]{:S(2)}) %collective-permute-start.5) | collective-permute-done | bytes 131104 | tf_op jit(solution)/shard_map/ppermute | solution.py:79
  70.6 2.1 collective-permute-done.6
  72.7 4.5 %collective-permute-start.11 = (bf16[1,8,64,128]{3,2,1,0:T(8,128)(2,1)S(1)}, bf16[1,8,64,128]{3,2,1,0:T(8,128)(2,1)S(1)}, u32[]{:S(2)}, u32[]{:S(2)}) collective-permute-start(bf16[1,8,64,128]{3,2,1,0:T(8,128)(2,1)S(1)} %copy-done.4), channel_id=1, source_target_pairs={{0,24},{2,26},{4,28},{6,30},{8,0},{10,2},{12,4},{14,6},{16,8},{18,... | collective-permute-start | bytes 393224 | tf_op jit(solution)/shard_map/ppermute | solution.py:79
  77.8 3.1 %collective-permute-start.12 = (bf16[1,8,64,128]{3,2,1,0:T(8,128)(2,1)S(1)}, bf16[1,8,64,128]{3,2,1,0:T(8,128)(2,1)S(1)}, u32[]{:S(2)}, u32[]{:S(2)}) collective-permute-start(bf16[1,8,64,128]{3,2,1,0:T(8,128)(2,1)S(1)} %copy-done.3), channel_id=1, source_target_pairs={{0,26},{2,28},{4,30},{6,0},{8,2},{10,4},{12,6},{14,8},{16,10},{18,... | collective-permute-start | bytes 393224 | tf_op jit(solution)/shard_map/ppermute | solution.py:79
  81.6 2.3 collective-permute-start.13
  84.6 2.0 collective-permute-start.14
  92.3 2.5 %gather_fusion = bf16[16,8,64,128]{3,2,1,0:T(8,128)(2,1)S(1)} fusion(bf16[16,8,64,128]{3,2,1,0:T(8,128)(2,1)} %bitcast.172, s32[1024]{0:T(1024)S(1)} %pad_clamp_fusion.1), kind=kCustom, calls=%fused_computation | custom fusion | bytes 4194368 | tf_op jit(solution)/shard_map/gather | solution.py:84
  94.8 24.0 %while.26 = (s32[]{:T(128)}, f32[256,256]{1,0:T(8,128)}, bf16[2,64,256,128]{3,2,1,0:T(8,128)(2,1)}, s32[2,64]{1,0:T(2,128)S(1)}, bf16[8,64,256]{2,0,1:T(8,128)(2...) while((s32[]{:T(128)}, f32[256,256]{1,0:T(8,128)}, ...), condition=%wide.region_4.5_spmd.clone, body=%wide.region_3.4_spmd.clone.sunk | while | flops 1362231808 | bytes 18614116 | solution.py:115
  95.6 5.7 %bitcast_dynamic-update-slice_fusion.23 = (bf16[2,64,256,128]{3,2,1,0:T(8,128)(2,1)}, bf16[64,256,128]{2,1,0:T(8,128)(2,1)}) fusion(bf16[2,64,256,128]{3,2,1,0:T(8,128)(2,1)} %get-tuple-element.303, s32[]{:T(128)} %get-tuple-element.301, bf16[2,64,64,128]{3,2,1,0:T(8,128)(2,1)S(1)} %get-tuple-element.314, ...), kind=kOutput, calls=%fused_computation.12.clone.1 | convolution fusion | flops 270532608 | bytes 11535360 | tf_op jit(solution)/shard_map/while/body/eval_jaxpr/sik,sim->skm/dot_general | solution.py:109
  101.3 5.4 %fusion.64 = f32[256,256]{1,0:T(8,128)} fusion(bf16[64,256,128]{2,1,0:T(8,128)(2,1)} %get-tuple-element.291, f32[256,256]{1,0:T(8,128)} %get-tuple-element.302, pred[]{:T(512)S(6)} %compare.48), kind=kOutput, calls=%fused_computation.17.clone.1 | convolution fusion | flops 1073872896 | bytes 4718593 | tf_op jit(solution)/shard_map/while/body/eval_jaxpr/skm,slm->kl/dot_general | solution.py:112
  107.5 5.8 %bitcast_dynamic-update-slice_fusion.23 = (bf16[2,64,256,128]{3,2,1,0:T(8,128)(2,1)}, bf16[64,256,128]{2,1,0:T(8,128)(2,1)}) fusion(bf16[2,64,256,128]{3,2,1,0:T(8,128)(2,1)} %get-tuple-element.303, s32[]{:T(128)} %get-tuple-element.301, bf16[2,64,64,128]{3,2,1,0:T(8,128)(2,1)S(1)} %get-tuple-element.314, ...), kind=kOutput, calls=%fused_computation.12.clone.1 | convolution fusion | flops 270532608 | bytes 11535360 | tf_op jit(solution)/shard_map/while/body/eval_jaxpr/sik,sim->skm/dot_general | solution.py:109
  113.4 5.4 %fusion.64 = f32[256,256]{1,0:T(8,128)} fusion(bf16[64,256,128]{2,1,0:T(8,128)(2,1)} %get-tuple-element.291, f32[256,256]{1,0:T(8,128)} %get-tuple-element.302, pred[]{:T(512)S(6)} %compare.48), kind=kOutput, calls=%fused_computation.17.clone.1 | convolution fusion | flops 1073872896 | bytes 4718593 | tf_op jit(solution)/shard_map/while/body/eval_jaxpr/skm,slm->kl/dot_general | solution.py:112
  118.8 1.8 copy.61
  120.7 23.5 %all-reduce.3.cloned.1.call-done = f32[256,256]{0,1:T(8,128)} async-done(((f32[256,256]{0,1:T(8,128)}), f32[256,256]{0,1:T(8,128)}) %all-reduce.3.cloned.1.call-update) | async-done | bytes 262160 | tf_op jit(solution)/shard_map/psum | solution.py:118
  146.3 11.7 %cholesky.49 = f32[128,128]{1,0:T(8,128)S(1)} custom-call(f32[128,128]{1,0:T(8,128)S(1)} %cholesky.115), custom_call_target="Cholesky" | custom-call | tf_op jit(solution)/shard_map/jit(cholesky)/cholesky | solution.py:120
  158.1 9.8 %custom-call.14 = f32[1,128,128]{1,2,0:T(8,128)S(1)} custom-call(f32[1,128,128]{2,1,0:T(8,128)S(1)} %get-tuple-element.193), custom_call_target="InvertDiagBlocksLowerTriangular" | custom-call | tf_op jit(solution)/shard_map/jit(cholesky)/cholesky | solution.py:120
  168.4 11.7 %cholesky.103 = f32[128,128]{1,0:T(8,128)S(1)} custom-call(f32[128,128]{1,0:T(8,128)S(1)} %convolution_subtract_fusion.1), custom_call_target="Cholesky" | custom-call | tf_op jit(solution)/shard_map/jit(cholesky)/cholesky | solution.py:120
  182.5 4.1 %while.25 = (s32[]{:T(128)}, f32[256,256]{0,1:T(8,128)S(1)}, s32[2,2]{1,0:T(2,128)S(1)}, f32[2,128,128]{2,1,0:T(8,128)S(1)}, s32[]{:T(128)}) while((s32[]{:T(128)}, f32[256,256]{0,1:T(8,128)S(1)}, s32[2,2]{1,0:T(2,128)S(1)}, f32[2,128,128]{2,1,0:T(8,128)S(1)}, s32[]{:T(128)}) %tuple.85), condition=%wide.while_cond, body=%wide.while_body.sunk | while | flops 2 | bytes 393321 | solution.py:122
  186.6 19.9 %custom-call.15 = f32[2,128,128]{1,2,0:T(8,128)S(1)} custom-call(f32[2,128,128]{2,1,0:T(8,128)S(1)} %get-tuple-element.70), custom_call_target="InvertDiagBlocksLowerTriangular" | custom-call | tf_op jit(solution)/shard_map/triangular_solve | solution.py:122
  207.5 10.5 %while.24 = (s32[]{:T(128)}, f32[2,64,128]{2,1,0:T(8,128)}, bf16[2,64,256,128]{3,2,1,0:T(8,128)(2,1)}, bf16[256,256]{1,0:T(8,128)(2,1)S(1)}, s32[]{:T(128)}) while((s32[]{:T(128)}, f32[2,64,128]{2,1,0:T(8,128)}, bf16[2,64,256,128]{3,2,1,0:T(8,128)(2,1)}, bf16[256,256]{1,0:T(8,128)(2,1)S(1)}, s32[]{:T(128)}) %tuple.88), condition=%wide.region_12.13_spmd, body=%wide.region_10.12_spmd.sunk | while | flops 1077936128 | bytes 4424765 | solution.py:130
  207.5 4.6 %multiply_reduce_fusion.2 = f32[64,128]{1,0:T(8,128)S(1)} fusion(bf16[2,64,256,128]{3,2,1,0:T(8,128)(2,1)} %get-tuple-element.344, s32[]{:T(128)} %get-tuple-element.337, bf16[256,256]{1,0:T(8,128)(2,1)S(1)} %get-tuple-element.345), kind=kOutput, calls=%fused_computation.4.clone.1 | convolution fusion | flops 1077927936 | bytes 4358656 | tf_op jit(solution)/shard_map/while/body/eval_jaxpr/kl,slm->skm/dot_general | solution.py:127
  212.8 4.6 %multiply_reduce_fusion.2 = f32[64,128]{1,0:T(8,128)S(1)} fusion(bf16[2,64,256,128]{3,2,1,0:T(8,128)(2,1)} %get-tuple-element.344, s32[]{:T(128)} %get-tuple-element.337, bf16[256,256]{1,0:T(8,128)(2,1)S(1)} %get-tuple-element.345), kind=kOutput, calls=%fused_computation.4.clone.1 | convolution fusion | flops 1077927936 | bytes 4358656 | tf_op jit(solution)/shard_map/while/body/eval_jaxpr/kl,slm->skm/dot_general | solution.py:127
  218.0 6.8 %all-to-all-start.1 = ((f32[16,8,128]{2,1,0:T(8,128)}), f32[16,8,128]{2,1,0:T(8,128)S(1)}, u32[]{:S(2)}, u32[]{:S(2)}) async-start(f32[16,8,128]{2,1,0:T(8,128)} %bitcast.53), calls=%async_computation.1 | async-start | bytes 131072 | tf_op jit(solution)/shard_map/all_to_all | solution.py:131
  224.9 7.5 %all-to-all-done.1 = f32[16,8,128]{2,1,0:T(8,128)S(1)} async-done(((f32[16,8,128]{2,1,0:T(8,128)}), f32[16,8,128]{2,1,0:T(8,128)S(1)}, u32[]{:S(2)}, u32[]{:S(2)}) %all-to-all-start.1) | async-done | bytes 65568 | tf_op jit(solution)/shard_map/all_to_all | solution.py:131
  (112 shorter events, 42.5 us)
Async XLA Ops:
  6.5 8.7 %copy-start = (bf16[64,64,128]{2,1,0:T(8,128)(2,1)S(1)}, bf16[64,64,128]{2,1,0:T(8,128)(2,1)}, u32[]{:S(2)}) copy-start(bf16[64,64,128]{2,1,0:T(8,128)(2,1)} %param.12) | copy-start | bytes 3145732
  14.5 0.7 copy-start.5
  23.6 19.0 %copy-start.1 = (bf16[1,512,256]{2,1,0:T(8,128)(2,1)S(1)}, bf16[1,512,256]{2,1,0:T(8,128)(2,1)}, u32[]{:S(2)}) copy-start(bf16[1,512,256]{2,1,0:T(8,128)(2,1)} %param.18) | copy-start | bytes 786436
  25.2 47.5 %copy-start.4 = (bf16[1,8,64,128]{3,2,1,0:T(8,128)(2,1)S(1)}, bf16[1,8,64,128]{3,2,1,0:T(8,128)(2,1)}, u32[]{:S(2)}) copy-start(bf16[1,8,64,128]{3,2,1,0:T(8,128)(2,1)} %get-tuple-element.179) | copy-start | bytes 393220
  25.2 52.7 %copy-start.3 = (bf16[1,8,64,128]{3,2,1,0:T(8,128)(2,1)S(1)}, bf16[1,8,64,128]{3,2,1,0:T(8,128)(2,1)}, u32[]{:S(2)}) copy-start(bf16[1,8,64,128]{3,2,1,0:T(8,128)(2,1)} %get-tuple-element.178) | copy-start | bytes 393220
  25.2 56.4 %copy-start.2 = (bf16[1,8,64,128]{3,2,1,0:T(8,128)(2,1)S(1)}, bf16[1,8,64,128]{3,2,1,0:T(8,128)(2,1)}, u32[]{:S(2)}) copy-start(bf16[1,8,64,128]{3,2,1,0:T(8,128)(2,1)} %get-tuple-element.177) | copy-start | bytes 393220
  25.2 26.3 %collective-permute-start = (bf16[1,8,64,128]{3,2,1,0:T(8,128)(2,1)}, bf16[1,8,64,128]{3,2,1,0:T(8,128)(2,1)S(1)}, u32[]{:S(2)}, u32[]{:S(2)}) collective-permute-start(bf16[1,8,64,128]{3,2,1,0:T(8,128)(2,1)} %get-tuple-element.190), channel_id=1, source_target_pairs={{0,2},{2,4},{4,6},{6,8},{8,10},{10,12},{12,14},{14,16},{16,18},{18... | collective-permute-start | bytes 393224 | tf_op jit(solution)/shard_map/ppermute | solution.py:79
  28.2 24.5 %collective-permute-start.1 = (bf16[1,8,64,128]{3,2,1,0:T(8,128)(2,1)}, bf16[1,8,64,128]{3,2,1,0:T(8,128)(2,1)S(1)}, u32[]{:S(2)}, u32[]{:S(2)}) collective-permute-start(bf16[1,8,64,128]{3,2,1,0:T(8,128)(2,1)} %get-tuple-element.189), channel_id=1, source_target_pairs={{0,4},{2,6},{4,8},{6,10},{8,12},{10,14},{12,16},{14,18},{16,20},{1... | collective-permute-start | bytes 393224 | tf_op jit(solution)/shard_map/ppermute | solution.py:79
  29.7 26.0 %collective-permute-start.2 = (bf16[1,8,64,128]{3,2,1,0:T(8,128)(2,1)}, bf16[1,8,64,128]{3,2,1,0:T(8,128)(2,1)S(1)}, u32[]{:S(2)}, u32[]{:S(2)}) collective-permute-start(bf16[1,8,64,128]{3,2,1,0:T(8,128)(2,1)} %get-tuple-element.188), channel_id=1, source_target_pairs={{0,6},{2,8},{4,10},{6,12},{8,14},{10,16},{12,18},{14,20},{16,22},{... | collective-permute-start | bytes 393224 | tf_op jit(solution)/shard_map/ppermute | solution.py:79
  32.2 25.6 %collective-permute-start.3 = (bf16[1,8,64,128]{3,2,1,0:T(8,128)(2,1)}, bf16[1,8,64,128]{3,2,1,0:T(8,128)(2,1)S(1)}, u32[]{:S(2)}, u32[]{:S(2)}) collective-permute-start(bf16[1,8,64,128]{3,2,1,0:T(8,128)(2,1)} %get-tuple-element.187), channel_id=1, source_target_pairs={{0,8},{2,10},{4,12},{6,14},{8,16},{10,18},{12,20},{14,22},{16,24},... | collective-permute-start | bytes 393224 | tf_op jit(solution)/shard_map/ppermute | solution.py:79
  33.8 26.3 %collective-permute-start.4 = (bf16[1,8,64,128]{3,2,1,0:T(8,128)(2,1)}, bf16[1,8,64,128]{3,2,1,0:T(8,128)(2,1)S(1)}, u32[]{:S(2)}, u32[]{:S(2)}) collective-permute-start(bf16[1,8,64,128]{3,2,1,0:T(8,128)(2,1)} %get-tuple-element.186), channel_id=1, source_target_pairs={{0,10},{2,12},{4,14},{6,16},{8,18},{10,20},{12,22},{14,24},{16,26}... | collective-permute-start | bytes 393224 | tf_op jit(solution)/shard_map/ppermute | solution.py:79
  37.0 13.2 %all-to-all-start = ((s32[16,1,8]{2,1,0:T(1,128)}), s32[16,1,8]{2,1,0:T(1,128)S(1)}, u32[]{:S(2)}, u32[]{:S(2)}) async-start(s32[16,1,8]{2,1,0:T(1,128)} %bitcast.6), calls=%async_computation | async-start | bytes 16384 | tf_op jit(solution)/shard_map/all_to_all | solution.py:90
  42.5 101.7 %all-reduce.3.cloned.1.call-start = ((), (), s32[]{:S(2)}) async-start(), calls=%async_computation.2 | async-start | bytes 524288 | tf_op jit(solution)/shard_map/psum | solution.py:118
  51.5 18.4 %collective-permute-start.5 = (bf16[1,8,64,128]{3,2,1,0:T(8,128)(2,1)}, bf16[1,8,64,128]{3,2,1,0:T(8,128)(2,1)S(1)}, u32[]{:S(2)}, u32[]{:S(2)}) collective-permute-start(bf16[1,8,64,128]{3,2,1,0:T(8,128)(2,1)} %get-tuple-element.185), channel_id=1, source_target_pairs={{0,12},{2,14},{4,16},{6,18},{8,20},{10,22},{12,24},{14,26},{16,28}... | collective-permute-start | bytes 393224 | tf_op jit(solution)/shard_map/ppermute | solution.py:79
  52.7 20.0 %collective-permute-start.6 = (bf16[1,8,64,128]{3,2,1,0:T(8,128)(2,1)}, bf16[1,8,64,128]{3,2,1,0:T(8,128)(2,1)S(1)}, u32[]{:S(2)}, u32[]{:S(2)}) collective-permute-start(bf16[1,8,64,128]{3,2,1,0:T(8,128)(2,1)} %get-tuple-element.184), channel_id=1, source_target_pairs={{0,14},{2,16},{4,18},{6,20},{8,22},{10,24},{12,26},{14,28},{16,30}... | collective-permute-start | bytes 393224 | tf_op jit(solution)/shard_map/ppermute | solution.py:79
  55.8 22.1 %collective-permute-start.7 = (bf16[1,8,64,128]{3,2,1,0:T(8,128)(2,1)}, bf16[1,8,64,128]{3,2,1,0:T(8,128)(2,1)S(1)}, u32[]{:S(2)}, u32[]{:S(2)}) collective-permute-start(bf16[1,8,64,128]{3,2,1,0:T(8,128)(2,1)} %get-tuple-element.183), channel_id=1, source_target_pairs={{0,16},{2,18},{4,20},{6,22},{8,24},{10,26},{12,28},{14,30},{16,0},... | collective-permute-start | bytes 393224 | tf_op jit(solution)/shard_map/ppermute | solution.py:79
  57.8 23.8 %collective-permute-start.8 = (bf16[1,8,64,128]{3,2,1,0:T(8,128)(2,1)}, bf16[1,8,64,128]{3,2,1,0:T(8,128)(2,1)S(1)}, u32[]{:S(2)}, u32[]{:S(2)}) collective-permute-start(bf16[1,8,64,128]{3,2,1,0:T(8,128)(2,1)} %get-tuple-element.182), channel_id=1, source_target_pairs={{0,18},{2,20},{4,22},{6,24},{8,26},{10,28},{12,30},{14,0},{16,2},{... | collective-permute-start | bytes 393224 | tf_op jit(solution)/shard_map/ppermute | solution.py:79
  60.0 24.6 %collective-permute-start.9 = (bf16[1,8,64,128]{3,2,1,0:T(8,128)(2,1)}, bf16[1,8,64,128]{3,2,1,0:T(8,128)(2,1)S(1)}, u32[]{:S(2)}, u32[]{:S(2)}) collective-permute-start(bf16[1,8,64,128]{3,2,1,0:T(8,128)(2,1)} %get-tuple-element.181), channel_id=1, source_target_pairs={{0,20},{2,22},{4,24},{6,26},{8,28},{10,30},{12,0},{14,2},{16,4},{1... | collective-permute-start | bytes 393224 | tf_op jit(solution)/shard_map/ppermute | solution.py:79
  69.9 17.4 %collective-permute-start.10 = (bf16[1,8,64,128]{3,2,1,0:T(8,128)(2,1)}, bf16[1,8,64,128]{3,2,1,0:T(8,128)(2,1)S(1)}, u32[]{:S(2)}, u32[]{:S(2)}) collective-permute-start(bf16[1,8,64,128]{3,2,1,0:T(8,128)(2,1)} %get-tuple-element.180), channel_id=1, source_target_pairs={{0,22},{2,24},{4,26},{6,28},{8,30},{10,0},{12,2},{14,4},{16,6},{18... | collective-permute-start | bytes 393224 | tf_op jit(solution)/shard_map/ppermute | solution.py:79
  72.7 15.3 %collective-permute-start.11 = (bf16[1,8,64,128]{3,2,1,0:T(8,128)(2,1)S(1)}, bf16[1,8,64,128]{3,2,1,0:T(8,128)(2,1)S(1)}, u32[]{:S(2)}, u32[]{:S(2)}) collective-permute-start(bf16[1,8,64,128]{3,2,1,0:T(8,128)(2,1)S(1)} %copy-done.4), channel_id=1, source_target_pairs={{0,24},{2,26},{4,28},{6,30},{8,0},{10,2},{12,4},{14,6},{16,8},{18,... | collective-permute-start | bytes 393224 | tf_op jit(solution)/shard_map/ppermute | solution.py:79
  77.8 10.8 %collective-permute-start.12 = (bf16[1,8,64,128]{3,2,1,0:T(8,128)(2,1)S(1)}, bf16[1,8,64,128]{3,2,1,0:T(8,128)(2,1)S(1)}, u32[]{:S(2)}, u32[]{:S(2)}) collective-permute-start(bf16[1,8,64,128]{3,2,1,0:T(8,128)(2,1)S(1)} %copy-done.3), channel_id=1, source_target_pairs={{0,26},{2,28},{4,30},{6,0},{8,2},{10,4},{12,6},{14,8},{16,10},{18,... | collective-permute-start | bytes 393224 | tf_op jit(solution)/shard_map/ppermute | solution.py:79
  81.6 7.7 %collective-permute-start.13 = (bf16[1,8,64,128]{3,2,1,0:T(8,128)(2,1)S(1)}, bf16[1,8,64,128]{3,2,1,0:T(8,128)(2,1)S(1)}, u32[]{:S(2)}, u32[]{:S(2)}) collective-permute-start(bf16[1,8,64,128]{3,2,1,0:T(8,128)(2,1)S(1)} %copy-done.2), channel_id=1, source_target_pairs={{0,28},{2,30},{4,0},{6,2},{8,4},{10,6},{12,8},{14,10},{16,12},{18,... | collective-permute-start | bytes 393224 | tf_op jit(solution)/shard_map/ppermute | solution.py:79
  84.6 7.0 %collective-permute-start.14 = (bf16[1,8,64,128]{3,2,1,0:T(8,128)(2,1)S(1)}, bf16[1,8,64,128]{3,2,1,0:T(8,128)(2,1)S(1)}, u32[]{:S(2)}, u32[]{:S(2)}) collective-permute-start(bf16[1,8,64,128]{3,2,1,0:T(8,128)(2,1)S(1)} %get-tuple-element.176), channel_id=1, source_target_pairs={{0,30},{2,0},{4,2},{6,4},{8,6},{10,8},{12,10},{14,12},{16,14},{18,... | collective-permute-start | bytes 393224 | tf_op jit(solution)/shard_map/ppermute | solution.py:79
  94.8 49.4 %copy-start.6 = (f32[1,256]{1,0:T(1,128)S(1)}, f32[1,256]{1,0:T(1,128)}, u32[]{:S(2)}) copy-start(f32[1,256]{1,0:T(1,128)} %param.19) | copy-start | bytes 3076
  218.0 14.4 %all-to-all-start.1 = ((f32[16,8,128]{2,1,0:T(8,128)}), f32[16,8,128]{2,1,0:T(8,128)S(1)}, u32[]{:S(2)}, u32[]{:S(2)}) async-start(f32[16,8,128]{2,1,0:T(8,128)} %bitcast.53), calls=%async_computation.1 | async-start | bytes 131072 | tf_op jit(solution)/shard_map/all_to_all | solution.py:131
Sparse Core Ops, SparseCore 0:
  120.8 23.3 all-reduce.2
